TPU v7x, 32 devices: a whole 2x2x4 slice. The times are simulated.
32 devices in a mesh: view: 2 (over core), gz: 8 (over z, y), gy: 2 (over x).
Axes of the slice: x: 2, y: 2, z: 4, core: 2. Of those that a mesh axis runs over, the one named last changes fastest.
Arguments:
- observed: float32 [2, 512, 32, 256], P('view', 'gz', 'gy'), may hold values from 0.5 to 4
- start: float32 [512, 32, 256], P('gz', 'gy'), may hold values from 0.5 to 2
- spread_z: float32 [2, 31], P('view'), may hold values from 0.05 to 1
- spread_y: float32 [2, 7], P('view'), may hold values from 0.1 to 1
- spread_x: float32 [2, 7], P('view'), may hold values from 0.1 to 1
Outputs:
- estimate: float32 [512, 32, 256], P('gz', 'gy')
All inputs are finite; a program needn't handle non-finite values.
Results may differ from a plain program's by a relative error of at most 0.0001.
Values sent between devices are 32-bit elements; how exact they have to be, the bound alone decides.
A program may use at most 64 MiB of HBM per device.

v0:
```python
import jax
import jax.numpy as jnp
from jax import lax
from jax.sharding import PartitionSpec as P

KZ = 31
KY = 7
KX = 7
ITERS = 2


def padded_2(x, sides, width):
    for axis, dim in sides:
        peers, length = (lax.axis_size(axis), x.shape[dim])
        up = [(i, (i + 1) % peers) for i in range(peers - 1)]
        down = [(j, i) for i, j in up]
        last = lax.slice_in_dim(x, length - width, length, axis=dim)
        first = lax.slice_in_dim(x, 0, width, axis=dim)
        before = lax.ppermute(last, axis, up)
        after = lax.ppermute(first, axis, down)
        x = jnp.concatenate([before, x, after], axis=dim)
    return x


def correlate(field, weights, along, margin):
    padding = [(0, 0), (0, 0), (0, 0)]
    padding[along] = (margin, margin)
    padded = jnp.pad(field, padding)
    taps = weights.shape[0]
    length = padded.shape[along] - taps + 1
    total = weights[0] * lax.slice_in_dim(padded, 0, length, 1, along)
    for offset in range(1, taps):
        total = total + weights[offset] * lax.slice_in_dim(
            padded, offset, offset + length, 1, along
        )
    return total


def blur_local(field, weight_z, weight_y, weight_x):
    padded = padded_2(field, (("gz", 0),), KZ // 2)
    field = correlate(padded, weight_z, 0, 0)
    padded = padded_2(field, (("gy", 1),), KY // 2)
    field = correlate(padded, weight_y, 1, 0)
    return correlate(field, weight_x, 2, KX // 2)


def on_device(observed, start, spread_z, spread_y, spread_x):
    recorded = observed[0]
    weight_z = spread_z[0] / jnp.sum(spread_z[0])
    weight_y = spread_y[0] / jnp.sum(spread_y[0])
    weight_x = spread_x[0] / jnp.sum(spread_x[0])
    estimate = start
    for sweep in range(ITERS):
        blurred = blur_local(estimate, weight_z, weight_y, weight_x)
        quotient = recorded / blurred
        correction = blur_local(quotient, weight_z[::-1], weight_y[::-1], weight_x[::-1])
        summed = lax.psum(correction, "view")
        estimate = estimate * (0.5 * summed)
    return estimate


def solution(mesh):
    return jax.shard_map(
        on_device,
        mesh=mesh,
        in_specs=(
            P("view", "gz", "gy", None),
            P("gz", "gy", None),
            P("view", None),
            P("view", None),
            P("view", None),
        ),
        out_specs=P("gz", "gy", None),
        check_vma=False,
    )
```

profile of v0, /device:TPU:0, one launch (start us, length us, event | category | flops | bytes accessed | tf_op | source)
XLA Modules:
  0.0 312.1 jit_solution(4010163259082128187)
XLA Ops:
  6.5 1.2 fusion.415
  7.7 4.9 %collective-permute-start = (f32[15,16,256]{2,1,0:T(8,128)S(1)}, f32[15,16,256]{2,1,0:T(8,128)S(1)}, u32[]{:S(2)}, u32[]{:S(2)}) collective-permute-start(f32[15,16,256]{2,1,0:T(8,128)S(1)} %get-tuple-element.21), channel_id=1, source_target_pairs={{0,2},{2,4},{4,6},{6,8},{8,10},{10,12},{12,14},{1,3},{3,5},{5,7},{... | collective-permute-start | bytes 737288 | tf_op jit(solution)/shard_map/ppermute | solution.py:19
  12.6 1.3 collective-permute-start.1
  13.9 1.3 reduce_sum.29
  15.2 0.7 reverse.11
  16.0 1.3 broadcast_divide_fusion
  17.3 0.7 fusion.422
  18.0 1.3 reduce_sum.28
  19.3 0.7 reverse.10
  20.0 1.3 broadcast_divide_fusion.2
  21.3 0.7 fusion.423
  22.0 1.3 reduce_sum.27
  23.3 0.7 reverse.9
  24.0 1.3 broadcast_divide_fusion.4
  25.7 23.5 %fusion.378 = f32[64,16,256]{2,1,0:T(8,128)S(1)} fusion(f32[79,16,256]{2,1,0:T(8,128)S(1)} %constant_dynamic-update-slice_fusion.2, f32[79,16,256]{2,1,0:T(8,128)S(1)} %get-tuple-element.19, f32[64,16,256]{2,1,0:T(8,128)S(1)} %copy-done, f32[]{:T(128)} %bitcast.39, f32[]{:T(128)} %bitcast.38, f32[]{:T(128)} %bitcast.37, f32[]{:T(128)} %bitcast.36, ...), kind=kLoop, calls=%fused_computation.617 | loop fusion | flops 15990784 | bytes 33554556 | tf_op jit(solution)/shard_map/add | solution.py:33
  49.3 1.3 collective-permute-start.3
  50.6 4.6 %collective-permute-start.2 = (f32[64,3,256]{2,1,0:T(4,128)S(1)}, f32[64,3,256]{2,1,0:T(4,128)S(1)}, u32[]{:S(2)}, u32[]{:S(2)}) collective-permute-start(f32[64,3,256]{2,1,0:T(4,128)S(1)} %get-tuple-element.17), channel_id=1, source_target_pairs={{0,1},{2,3},{4,5},{6,7},{8,9},{10,11},{12,13},{14,15},{16,17},{18,... | collective-permute-start | bytes 589832 | tf_op jit(solution)/shard_map/ppermute | solution.py:19
  55.2 0.7 fusion.421
  55.9 0.7 fusion.420
  56.5 2.4 collective-permute-done.3
  59.0 1.2 collective-permute-done.2
  60.2 5.4 %fusion.45 = f32[64,16,256]{2,1,0:T(8,128)S(1)} fusion(f32[64,16,256]{2,1,0:T(8,128)S(1)} %fusion.378, f32[64,3,256]{2,1,0:T(4,128)S(1)} %collective-permute-done.3, f32[64,3,256]{2,1,0:T(4,128)S(1)} %collective-permute-done.2, f32[]{:T(128)} %bitcast.45, f32[]{:T(128)} %bitcast.44, f32[]{:T(128)} %bitcast.43, f32[]{:T(128)} %bitcast.42, f32[]{:T(128)} %bitcast.41, ...), kind=kLoop, calls=%fused_computation.269 | loop fusion | flops 4980736 | bytes 2490396 | tf_op jit(solution)/shard_map/add | solution.py:33
  65.6 6.1 %fusion.321 = f32[64,16,256]{2,1,0:T(8,128)S(1)} fusion(f32[64,16,256]{2,1,0:T(8,128)S(1)} %fusion.45, f32[1,64,16,256]{3,2,1,0:T(8,128)S(1)} %copy-done.1, f32[]{:T(128)} %bitcast.51, f32[]{:T(128)} %bitcast.50, f32[]{:T(128)} %bitcast.49, f32[]{:T(128)} %bitcast.48, f32[]{:T(128)} %bitcast.47, f32[]{:T(128)} %bitcast.46, f32[]{:T(128)} %bitcast.7), kind=kLoop, calls=%fused_computation.545 | loop fusion | flops 3670016 | bytes 3145756 | tf_op jit(solution)/shard_map/div | solution.py:55
  71.7 1.3 collective-permute-start.5
  73.0 4.9 %collective-permute-start.4 = (f32[15,16,256]{2,1,0:T(8,128)S(1)}, f32[15,16,256]{2,1,0:T(8,128)S(1)}, u32[]{:S(2)}, u32[]{:S(2)}) collective-permute-start(f32[15,16,256]{2,1,0:T(8,128)S(1)} %get-tuple-element.15), channel_id=1, source_target_pairs={{0,2},{2,4},{4,6},{6,8},{8,10},{10,12},{12,14},{1,3},{3,5},{5,7},{... | collective-permute-start | bytes 737288 | tf_op jit(solution)/shard_map/ppermute | solution.py:19
  78.0 0.7 fusion.419
  78.7 0.7 fusion.418
  79.4 0.9 collective-permute-done.5
  80.3 5.4 %collective-permute-done.4 = f32[15,16,256]{2,1,0:T(8,128)S(1)} collective-permute-done((f32[15,16,256]{2,1,0:T(8,128)S(1)}, f32[15,16,256]{2,1,0:T(8,128)S(1)}, u32[]{:S(2)}, u32[]{:S(2)}) %collective-permute-start.4) | collective-permute-done | bytes 245792 | tf_op jit(solution)/shard_map/ppermute | solution.py:19
  85.7 23.9 %fusion.231 = f32[64,16,256]{2,1,0:T(8,128)S(1)} fusion(f32[64,16,256]{2,1,0:T(8,128)S(1)} %fusion.321, f32[15,16,256]{2,1,0:T(8,128)S(1)} %collective-permute-done.5, f32[15,16,256]{2,1,0:T(8,128)S(1)} %collective-permute-done.4, f32[]{:T(128)} %bitcast.81, f32[]{:T(128)} %bitcast.80, f32[]{:T(128)} %bitcast.79, f32[]{:T(128)} %bitcast.78, f32[]{:T(128)} %bitcast.77, ...), kind=kLoop, calls=%fused_computation.455 | loop fusion | flops 23855104 | bytes 2588796 | tf_op jit(solution)/shard_map/add | solution.py:33
  109.7 1.3 collective-permute-start.7
  111.0 4.6 %collective-permute-start.6 = (f32[64,3,256]{2,1,0:T(4,128)S(1)}, f32[64,3,256]{2,1,0:T(4,128)S(1)}, u32[]{:S(2)}, u32[]{:S(2)}) collective-permute-start(f32[64,3,256]{2,1,0:T(4,128)S(1)} %get-tuple-element.13), channel_id=1, source_target_pairs={{0,1},{2,3},{4,5},{6,7},{8,9},{10,11},{12,13},{14,15},{16,17},{18,... | collective-permute-start | bytes 589832 | tf_op jit(solution)/shard_map/ppermute | solution.py:19
  115.6 0.7 fusion.417
  116.2 0.6 fusion.416
  116.9 2.9 collective-permute-done.7
  119.8 1.2 collective-permute-done.6
  121.0 5.4 %fusion.31 = f32[64,16,256]{2,1,0:T(8,128)S(1)} fusion(f32[64,16,256]{2,1,0:T(8,128)S(1)} %fusion.231, f32[64,3,256]{2,1,0:T(4,128)S(1)} %collective-permute-done.7, f32[64,3,256]{2,1,0:T(4,128)S(1)} %collective-permute-done.6, f32[]{:T(128)} %bitcast.87, f32[]{:T(128)} %bitcast.86, f32[]{:T(128)} %bitcast.85, f32[]{:T(128)} %bitcast.84, f32[]{:T(128)} %bitcast.83, ...), kind=kLoop, calls=%fused_computation.255 | loop fusion | flops 4980736 | bytes 2490396 | tf_op jit(solution)/shard_map/add | solution.py:33
  126.5 6.8 %fusion.333 = f32[64,16,256]{2,1,0:T(8,128)} fusion(f32[64,16,256]{2,1,0:T(8,128)S(1)} %fusion.31, f32[]{:T(128)} %bitcast.93, f32[]{:T(128)} %bitcast.92, f32[]{:T(128)} %bitcast.91, f32[]{:T(128)} %bitcast.90, f32[]{:T(128)} %bitcast.89, f32[]{:T(128)} %bitcast.88, f32[]{:T(128)} %bitcast.1), kind=kLoop, calls=%fused_computation.557 | loop fusion | flops 3407872 | bytes 2097180 | tf_op jit(solution)/shard_map/add | solution.py:33
  133.4 21.7 %all-reduce.7.cloned.1.call-done = f32[64,16,256]{2,1,0:T(8,128)} async-done(((f32[64,16,256]{2,1,0:T(8,128)}), f32[64,16,256]{2,1,0:T(8,128)}) %all-reduce.7.cloned.1.call-update) | async-done | bytes 1048592 | tf_op jit(solution)/shard_map/psum | solution.py:57
  155.1 1.4 multiply_multiply_fusion.1
  156.6 1.3 collective-permute-start.9
  157.9 4.7 %collective-permute-start.8 = (f32[15,16,256]{2,1,0:T(8,128)S(1)}, f32[15,16,256]{2,1,0:T(8,128)S(1)}, u32[]{:S(2)}, u32[]{:S(2)}) collective-permute-start(f32[15,16,256]{2,1,0:T(8,128)S(1)} %get-tuple-element.11), channel_id=1, source_target_pairs={{0,2},{2,4},{4,6},{6,8},{8,10},{10,12},{12,14},{1,3},{3,5},{5,7},{... | collective-permute-start | bytes 737288 | tf_op jit(solution)/shard_map/ppermute | solution.py:19
  162.6 4.0 %collective-permute-done.9 = f32[15,16,256]{2,1,0:T(8,128)S(1)} collective-permute-done((f32[15,16,256]{2,1,0:T(8,128)S(1)}, f32[15,16,256]{2,1,0:T(8,128)S(1)}, u32[]{:S(2)}, u32[]{:S(2)}) %collective-permute-start.9) | collective-permute-done | bytes 245792 | tf_op jit(solution)/shard_map/ppermute | solution.py:20
  166.6 5.4 %collective-permute-done.8 = f32[15,16,256]{2,1,0:T(8,128)S(1)} collective-permute-done((f32[15,16,256]{2,1,0:T(8,128)S(1)}, f32[15,16,256]{2,1,0:T(8,128)S(1)}, u32[]{:S(2)}, u32[]{:S(2)}) %collective-permute-start.8) | collective-permute-done | bytes 245792 | tf_op jit(solution)/shard_map/ppermute | solution.py:19
  172.0 23.7 %fusion.145 = f32[64,16,256]{2,1,0:T(8,128)S(1)} fusion(f32[64,16,256]{2,1,0:T(8,128)S(1)} %multiply_multiply_fusion.1, f32[15,16,256]{2,1,0:T(8,128)S(1)} %collective-permute-done.9, f32[15,16,256]{2,1,0:T(8,128)S(1)} %collective-permute-done.8, f32[]{:T(128)} %bitcast.39, f32[]{:T(128)} %bitcast.38, f32[]{:T(128)} %bitcast.37, f32[]{:T(128)} %bitcast.36, ...), kind=kLoop, calls=%fused_computation.369 | loop fusion | flops 23855104 | bytes 2588796 | tf_op jit(solution)/shard_map/add | solution.py:33
  195.9 1.3 collective-permute-start.11
  197.2 4.6 %collective-permute-start.10 = (f32[64,3,256]{2,1,0:T(4,128)S(1)}, f32[64,3,256]{2,1,0:T(4,128)S(1)}, u32[]{:S(2)}, u32[]{:S(2)}) collective-permute-start(f32[64,3,256]{2,1,0:T(4,128)S(1)} %get-tuple-element.9), channel_id=1, source_target_pairs={{0,1},{2,3},{4,5},{6,7},{8,9},{10,11},{12,13},{14,15},{16,17},{18,... | collective-permute-start | bytes 589832 | tf_op jit(solution)/shard_map/ppermute | solution.py:19
  201.8 4.2 %collective-permute-done.11 = f32[64,3,256]{2,1,0:T(4,128)S(1)} collective-permute-done((f32[64,3,256]{2,1,0:T(4,128)S(1)}, f32[64,3,256]{2,1,0:T(4,128)S(1)}, u32[]{:S(2)}, u32[]{:S(2)}) %collective-permute-start.11) | collective-permute-done | bytes 196640 | tf_op jit(solution)/shard_map/ppermute | solution.py:20
  206.0 1.2 collective-permute-done.10
  207.2 5.3 %fusion.17 = f32[64,16,256]{2,1,0:T(8,128)S(1)} fusion(f32[64,16,256]{2,1,0:T(8,128)S(1)} %fusion.145, f32[64,3,256]{2,1,0:T(4,128)S(1)} %collective-permute-done.11, f32[64,3,256]{2,1,0:T(4,128)S(1)} %collective-permute-done.10, f32[]{:T(128)} %bitcast.45, f32[]{:T(128)} %bitcast.44, f32[]{:T(128)} %bitcast.43, f32[]{:T(128)} %bitcast.42, f32[]{:T(128)} %bitcast.41, ...), kind=kLoop, calls=%fused_computation.241 | loop fusion | flops 4980736 | bytes 2490396 | tf_op jit(solution)/shard_map/add | solution.py:33
  212.5 6.1 %fusion.346 = f32[64,16,256]{2,1,0:T(8,128)S(1)} fusion(f32[64,16,256]{2,1,0:T(8,128)S(1)} %fusion.17, f32[1,64,16,256]{3,2,1,0:T(8,128)S(1)} %copy-done.1, f32[]{:T(128)} %bitcast.51, f32[]{:T(128)} %bitcast.50, f32[]{:T(128)} %bitcast.49, f32[]{:T(128)} %bitcast.48, f32[]{:T(128)} %bitcast.47, f32[]{:T(128)} %bitcast.46, f32[]{:T(128)} %bitcast.7), kind=kLoop, calls=%fused_computation.570 | loop fusion | flops 3670016 | bytes 3145756 | tf_op jit(solution)/shard_map/div | solution.py:55
  218.7 1.3 collective-permute-start.13
  220.0 5.0 %collective-permute-start.12 = (f32[15,16,256]{2,1,0:T(8,128)S(1)}, f32[15,16,256]{2,1,0:T(8,128)S(1)}, u32[]{:S(2)}, u32[]{:S(2)}) collective-permute-start(f32[15,16,256]{2,1,0:T(8,128)S(1)} %get-tuple-element.7), channel_id=1, source_target_pairs={{0,2},{2,4},{4,6},{6,8},{8,10},{10,12},{12,14},{1,3},{3,5},{5,7},{... | collective-permute-start | bytes 737288 | tf_op jit(solution)/shard_map/ppermute | solution.py:19
  225.0 3.1 collective-permute-done.13
  228.1 5.4 %collective-permute-done.12 = f32[15,16,256]{2,1,0:T(8,128)S(1)} collective-permute-done((f32[15,16,256]{2,1,0:T(8,128)S(1)}, f32[15,16,256]{2,1,0:T(8,128)S(1)}, u32[]{:S(2)}, u32[]{:S(2)}) %collective-permute-start.12) | collective-permute-done | bytes 245792 | tf_op jit(solution)/shard_map/ppermute | solution.py:19
  233.5 23.9 %fusion.59 = f32[64,16,256]{2,1,0:T(8,128)S(1)} fusion(f32[64,16,256]{2,1,0:T(8,128)S(1)} %fusion.346, f32[15,16,256]{2,1,0:T(8,128)S(1)} %collective-permute-done.13, f32[15,16,256]{2,1,0:T(8,128)S(1)} %collective-permute-done.12, f32[]{:T(128)} %bitcast.81, f32[]{:T(128)} %bitcast.80, f32[]{:T(128)} %bitcast.79, f32[]{:T(128)} %bitcast.78, f32[]{:T(128)} %bitcast.77, ...), kind=kLoop, calls=%fused_computation.283 | loop fusion | flops 23855104 | bytes 2588796 | tf_op jit(solution)/shard_map/add | solution.py:33
  257.5 1.3 collective-permute-start.15
  258.8 4.6 %collective-permute-start.14 = (f32[64,3,256]{2,1,0:T(4,128)S(1)}, f32[64,3,256]{2,1,0:T(4,128)S(1)}, u32[]{:S(2)}, u32[]{:S(2)}) collective-permute-start(f32[64,3,256]{2,1,0:T(4,128)S(1)} %get-tuple-element.5), channel_id=1, source_target_pairs={{0,1},{2,3},{4,5},{6,7},{8,9},{10,11},{12,13},{14,15},{16,17},{18,... | collective-permute-start | bytes 589832 | tf_op jit(solution)/shard_map/ppermute | solution.py:19
  263.4 4.4 %collective-permute-done.15 = f32[64,3,256]{2,1,0:T(4,128)S(1)} collective-permute-done((f32[64,3,256]{2,1,0:T(4,128)S(1)}, f32[64,3,256]{2,1,0:T(4,128)S(1)}, u32[]{:S(2)}, u32[]{:S(2)}) %collective-permute-start.15) | collective-permute-done | bytes 196640 | tf_op jit(solution)/shard_map/ppermute | solution.py:20
  267.7 1.2 collective-permute-done.14
  268.9 5.4 %fusion.3 = f32[64,16,256]{2,1,0:T(8,128)S(1)} fusion(f32[64,16,256]{2,1,0:T(8,128)S(1)} %fusion.59, f32[64,3,256]{2,1,0:T(4,128)S(1)} %collective-permute-done.15, f32[64,3,256]{2,1,0:T(4,128)S(1)} %collective-permute-done.14, f32[]{:T(128)} %bitcast.87, f32[]{:T(128)} %bitcast.86, f32[]{:T(128)} %bitcast.85, f32[]{:T(128)} %bitcast.84, f32[]{:T(128)} %bitcast.83, ...), kind=kLoop, calls=%fused_computation.227 | loop fusion | flops 4980736 | bytes 2490396 | tf_op jit(solution)/shard_map/add | solution.py:33
  274.4 6.8 %fusion.358 = f32[64,16,256]{2,1,0:T(8,128)} fusion(f32[64,16,256]{2,1,0:T(8,128)S(1)} %fusion.3, f32[]{:T(128)} %bitcast.93, f32[]{:T(128)} %bitcast.92, f32[]{:T(128)} %bitcast.91, f32[]{:T(128)} %bitcast.90, f32[]{:T(128)} %bitcast.89, f32[]{:T(128)} %bitcast.88, f32[]{:T(128)} %bitcast.1), kind=kLoop, calls=%fused_computation.582 | loop fusion | flops 3407872 | bytes 2097180 | tf_op jit(solution)/shard_map/add | solution.py:33
  281.2 21.6 %all-reduce.9.cloned.1.call-done = f32[64,16,256]{2,1,0:T(8,128)} async-done(((f32[64,16,256]{2,1,0:T(8,128)}), f32[64,16,256]{2,1,0:T(8,128)}) %all-reduce.9.cloned.1.call-update) | async-done | bytes 1048592 | tf_op jit(solution)/shard_map/psum | solution.py:57
  302.8 2.4 multiply_multiply_fusion
  (20 shorter events, 0.9 us)
Async XLA Ops:
  6.5 18.8 %copy-start = (f32[64,16,256]{2,1,0:T(8,128)S(1)}, f32[64,16,256]{2,1,0:T(8,128)}, u32[]{:S(2)}) copy-start(f32[64,16,256]{2,1,0:T(8,128)} %param.6) | copy-start | bytes 3145732
  6.5 148.5 %all-reduce.7.cloned.1.call-start = ((), (), s32[]{:S(2)}) async-start(), calls=%async_computation | async-start | bytes 2097152 | tf_op jit(solution)/shard_map/psum | solution.py:57
  7.7 17.6 %collective-permute-start = (f32[15,16,256]{2,1,0:T(8,128)S(1)}, f32[15,16,256]{2,1,0:T(8,128)S(1)}, u32[]{:S(2)}, u32[]{:S(2)}) collective-permute-start(f32[15,16,256]{2,1,0:T(8,128)S(1)} %get-tuple-element.21), channel_id=1, source_target_pairs={{0,2},{2,4},{4,6},{6,8},{8,10},{10,12},{12,14},{1,3},{3,5},{5,7},{... | collective-permute-start | bytes 737288 | tf_op jit(solution)/shard_map/ppermute | solution.py:19
  12.6 13.0 %collective-permute-start.1 = (f32[15,16,256]{2,1,0:T(8,128)S(1)}, f32[15,16,256]{2,1,0:T(8,128)S(1)}, u32[]{:S(2)}, u32[]{:S(2)}) collective-permute-start(f32[15,16,256]{2,1,0:T(8,128)S(1)} %get-tuple-element.22), channel_id=1, source_target_pairs={{2,0},{4,2},{6,4},{8,6},{10,8},{12,10},{14,12},{3,1},{5,3},{7,5},{... | collective-permute-start | bytes 737288 | tf_op jit(solution)/shard_map/ppermute | solution.py:20
  49.3 9.7 %collective-permute-start.3 = (f32[64,3,256]{2,1,0:T(4,128)S(1)}, f32[64,3,256]{2,1,0:T(4,128)S(1)}, u32[]{:S(2)}, u32[]{:S(2)}) collective-permute-start(f32[64,3,256]{2,1,0:T(4,128)S(1)} %get-tuple-element.18), channel_id=1, source_target_pairs={{1,0},{3,2},{5,4},{7,6},{9,8},{11,10},{13,12},{15,14},{17,16},{19,... | collective-permute-start | bytes 589832 | tf_op jit(solution)/shard_map/ppermute | solution.py:20
  50.6 9.6 %collective-permute-start.2 = (f32[64,3,256]{2,1,0:T(4,128)S(1)}, f32[64,3,256]{2,1,0:T(4,128)S(1)}, u32[]{:S(2)}, u32[]{:S(2)}) collective-permute-start(f32[64,3,256]{2,1,0:T(4,128)S(1)} %get-tuple-element.17), channel_id=1, source_target_pairs={{0,1},{2,3},{4,5},{6,7},{8,9},{10,11},{12,13},{14,15},{16,17},{18,... | collective-permute-start | bytes 589832 | tf_op jit(solution)/shard_map/ppermute | solution.py:19
  60.2 5.4 %copy-start.1 = (f32[1,64,16,256]{3,2,1,0:T(8,128)S(1)}, f32[1,64,16,256]{3,2,1,0:T(8,128)}, u32[]{:S(2)}) copy-start(f32[1,64,16,256]{3,2,1,0:T(8,128)} %param.5) | copy-start | bytes 3145732
  71.7 8.5 %collective-permute-start.5 = (f32[15,16,256]{2,1,0:T(8,128)S(1)}, f32[15,16,256]{2,1,0:T(8,128)S(1)}, u32[]{:S(2)}, u32[]{:S(2)}) collective-permute-start(f32[15,16,256]{2,1,0:T(8,128)S(1)} %get-tuple-element.16), channel_id=1, source_target_pairs={{2,0},{4,2},{6,4},{8,6},{10,8},{12,10},{14,12},{3,1},{5,3},{7,5},{... | collective-permute-start | bytes 737288 | tf_op jit(solution)/shard_map/ppermute | solution.py:20
  73.0 12.6 %collective-permute-start.4 = (f32[15,16,256]{2,1,0:T(8,128)S(1)}, f32[15,16,256]{2,1,0:T(8,128)S(1)}, u32[]{:S(2)}, u32[]{:S(2)}) collective-permute-start(f32[15,16,256]{2,1,0:T(8,128)S(1)} %get-tuple-element.15), channel_id=1, source_target_pairs={{0,2},{2,4},{4,6},{6,8},{8,10},{10,12},{12,14},{1,3},{3,5},{5,7},{... | collective-permute-start | bytes 737288 | tf_op jit(solution)/shard_map/ppermute | solution.py:19
  109.7 10.1 %collective-permute-start.7 = (f32[64,3,256]{2,1,0:T(4,128)S(1)}, f32[64,3,256]{2,1,0:T(4,128)S(1)}, u32[]{:S(2)}, u32[]{:S(2)}) collective-permute-start(f32[64,3,256]{2,1,0:T(4,128)S(1)} %get-tuple-element.14), channel_id=1, source_target_pairs={{1,0},{3,2},{5,4},{7,6},{9,8},{11,10},{13,12},{15,14},{17,16},{19,... | collective-permute-start | bytes 589832 | tf_op jit(solution)/shard_map/ppermute | solution.py:20
  111.0 10.0 %collective-permute-start.6 = (f32[64,3,256]{2,1,0:T(4,128)S(1)}, f32[64,3,256]{2,1,0:T(4,128)S(1)}, u32[]{:S(2)}, u32[]{:S(2)}) collective-permute-start(f32[64,3,256]{2,1,0:T(4,128)S(1)} %get-tuple-element.13), channel_id=1, source_target_pairs={{0,1},{2,3},{4,5},{6,7},{8,9},{10,11},{12,13},{14,15},{16,17},{18,... | collective-permute-start | bytes 589832 | tf_op jit(solution)/shard_map/ppermute | solution.py:19
  133.3 169.5 %all-reduce.9.cloned.1.call-start = ((), (), s32[]{:S(2)}) async-start(), calls=%async_computation.1 | async-start | bytes 2097152 | tf_op jit(solution)/shard_map/psum | solution.py:57
  156.6 10.1 %collective-permute-start.9 = (f32[15,16,256]{2,1,0:T(8,128)S(1)}, f32[15,16,256]{2,1,0:T(8,128)S(1)}, u32[]{:S(2)}, u32[]{:S(2)}) collective-permute-start(f32[15,16,256]{2,1,0:T(8,128)S(1)} %get-tuple-element.12), channel_id=1, source_target_pairs={{2,0},{4,2},{6,4},{8,6},{10,8},{12,10},{14,12},{3,1},{5,3},{7,5},{... | collective-permute-start | bytes 737288 | tf_op jit(solution)/shard_map/ppermute | solution.py:20
  157.9 14.2 %collective-permute-start.8 = (f32[15,16,256]{2,1,0:T(8,128)S(1)}, f32[15,16,256]{2,1,0:T(8,128)S(1)}, u32[]{:S(2)}, u32[]{:S(2)}) collective-permute-start(f32[15,16,256]{2,1,0:T(8,128)S(1)} %get-tuple-element.11), channel_id=1, source_target_pairs={{0,2},{2,4},{4,6},{6,8},{8,10},{10,12},{12,14},{1,3},{3,5},{5,7},{... | collective-permute-start | bytes 737288 | tf_op jit(solution)/shard_map/ppermute | solution.py:19
  195.9 10.1 %collective-permute-start.11 = (f32[64,3,256]{2,1,0:T(4,128)S(1)}, f32[64,3,256]{2,1,0:T(4,128)S(1)}, u32[]{:S(2)}, u32[]{:S(2)}) collective-permute-start(f32[64,3,256]{2,1,0:T(4,128)S(1)} %get-tuple-element.10), channel_id=1, source_target_pairs={{1,0},{3,2},{5,4},{7,6},{9,8},{11,10},{13,12},{15,14},{17,16},{19,... | collective-permute-start | bytes 589832 | tf_op jit(solution)/shard_map/ppermute | solution.py:20
  197.2 10.0 %collective-permute-start.10 = (f32[64,3,256]{2,1,0:T(4,128)S(1)}, f32[64,3,256]{2,1,0:T(4,128)S(1)}, u32[]{:S(2)}, u32[]{:S(2)}) collective-permute-start(f32[64,3,256]{2,1,0:T(4,128)S(1)} %get-tuple-element.9), channel_id=1, source_target_pairs={{0,1},{2,3},{4,5},{6,7},{8,9},{10,11},{12,13},{14,15},{16,17},{18,... | collective-permute-start | bytes 589832 | tf_op jit(solution)/shard_map/ppermute | solution.py:19
  218.7 9.4 %collective-permute-start.13 = (f32[15,16,256]{2,1,0:T(8,128)S(1)}, f32[15,16,256]{2,1,0:T(8,128)S(1)}, u32[]{:S(2)}, u32[]{:S(2)}) collective-permute-start(f32[15,16,256]{2,1,0:T(8,128)S(1)} %get-tuple-element.8), channel_id=1, source_target_pairs={{2,0},{4,2},{6,4},{8,6},{10,8},{12,10},{14,12},{3,1},{5,3},{7,5},{... | collective-permute-start | bytes 737288 | tf_op jit(solution)/shard_map/ppermute | solution.py:20
  220.0 13.5 %collective-permute-start.12 = (f32[15,16,256]{2,1,0:T(8,128)S(1)}, f32[15,16,256]{2,1,0:T(8,128)S(1)}, u32[]{:S(2)}, u32[]{:S(2)}) collective-permute-start(f32[15,16,256]{2,1,0:T(8,128)S(1)} %get-tuple-element.7), channel_id=1, source_target_pairs={{0,2},{2,4},{4,6},{6,8},{8,10},{10,12},{12,14},{1,3},{3,5},{5,7},{... | collective-permute-start | bytes 737288 | tf_op jit(solution)/shard_map/ppermute | solution.py:19
  257.5 10.2 %collective-permute-start.15 = (f32[64,3,256]{2,1,0:T(4,128)S(1)}, f32[64,3,256]{2,1,0:T(4,128)S(1)}, u32[]{:S(2)}, u32[]{:S(2)}) collective-permute-start(f32[64,3,256]{2,1,0:T(4,128)S(1)} %get-tuple-element.6), channel_id=1, source_target_pairs={{1,0},{3,2},{5,4},{7,6},{9,8},{11,10},{13,12},{15,14},{17,16},{19,... | collective-permute-start | bytes 589832 | tf_op jit(solution)/shard_map/ppermute | solution.py:20
  258.8 10.1 %collective-permute-start.14 = (f32[64,3,256]{2,1,0:T(4,128)S(1)}, f32[64,3,256]{2,1,0:T(4,128)S(1)}, u32[]{:S(2)}, u32[]{:S(2)}) collective-permute-start(f32[64,3,256]{2,1,0:T(4,128)S(1)} %get-tuple-element.5), channel_id=1, source_target_pairs={{0,1},{2,3},{4,5},{6,7},{8,9},{10,11},{12,13},{14,15},{16,17},{18,... | collective-permute-start | bytes 589832 | tf_op jit(solution)/shard_map/ppermute | solution.py:19
Sparse Core Ops, SparseCore 0:
  133.4 21.5 all-reduce.6
  281.4 21.4 all-reduce.8
where the time goes:
time: 314 us; the launch traced here: 312 us
  other arithmetic  154 us (49%)
  waiting for transfers between devices  86.3 us (27%)
  starting transfers between devices  48.3 us (15%)
  between operations  13.7 us (4%)
  local copies, waits for them, and re-layouts  9.71 us (3%)
    add x10, other arithmetic, correlate(): total + weights[offset] * lax.slice_in_dim(padded, offset, offset + lengt...  130 us
    psum x2, waiting for transfers between devices, on_device(): summed = lax.psum(correction, 'view')  43.3 us
    ppermute x8, starting transfers between devices, padded_2(): before = lax.ppermute(last, axis, up)  37.9 us
    ppermute x8, waiting for transfers between devices, padded_2(): after = lax.ppermute(first, axis, down)  21.9 us
    ppermute x8, waiting for transfers between devices, padded_2(): before = lax.ppermute(last, axis, up)  21 us
    div x2, other arithmetic, on_device(): quotient = recorded / blurred  12.2 us
    ppermute x8, starting transfers between devices, padded_2(): after = lax.ppermute(first, axis, down)  10.3 us
  transfers between devices with their start and end apart: 18, of which 16 were waited for; matrix products, arithmetic and copies ran while one was open for 5% of the time, Pallas kernels for 0%

commit v1 on v0

--- a/solution.py
+++ b/solution.py
@@ -54,7 +54,8 @@
         blurred = blur_local(estimate, weight_z, weight_y, weight_x)
         quotient = recorded / blurred
         correction = blur_local(quotient, weight_z[::-1], weight_y[::-1], weight_x[::-1])
-        summed = lax.psum(correction, "view")
+        parts = lax.all_gather(correction, "view", axis=0, tiled=False)
+        summed = parts.sum(axis=0)
         estimate = estimate * (0.5 * summed)
     return estimate
 

time: 314 us -> 299 us (0.952)
  starting transfers between devices: 48.3 us -> 37.8 us
  waiting for transfers between devices: 86.3 us -> 80.1 us
    psum x2 -> x0, waiting for transfers between devices: 43.3 us -> none  [on_device(): summed = lax.psum(correction, 'view')]
    all_gather x0 -> x2, waiting for transfers between devices: none -> 29.3 us  [on_device(): parts = lax.all_gather(correction, 'view', axis=0, tiled=False)]
    ppermute x8, starting transfers between devices: 37.9 us -> 27.1 us  [padded_2(): before = lax.ppermute(last, axis, up)]
    ppermute x8, waiting for transfers between devices: 21 us -> 25.5 us  [padded_2(): before = lax.ppermute(last, axis, up)]
    reduce_sum x0 -> x2, other arithmetic: none -> 3.78 us  [on_device(): summed = parts.sum(axis=0)]
    ppermute x8, waiting for transfers between devices: 21.9 us -> 25.2 us  [padded_2(): after = lax.ppermute(first, axis, down)]
  transfers between devices with their start and end apart: 18 -> 18, of which waited for: 16 -> 15; matrix products, arithmetic and copies ran while one was open for 5% -> 5% of each run, Pallas kernels for 0% -> 0%
where the time goes in v1:
time: 299 us; the launch traced here: 297 us
  other arithmetic  155 us (52%)
  waiting for transfers between devices  80.1 us (27%)
  starting transfers between devices  37.8 us (13%)
  between operations  13.8 us (5%)
  local copies, waits for them, and re-layouts  9.74 us (3%)
    add x10, other arithmetic, correlate(): total + weights[offset] * lax.slice_in_dim(padded, offset, offset + lengt...  130 us
    all_gather x2, waiting for transfers between devices, on_device(): parts = lax.all_gather(correction, 'view', axis=0, tiled=False)  29.3 us
    ppermute x8, starting transfers between devices, padded_2(): before = lax.ppermute(last, axis, up)  27.1 us
    ppermute x8, waiting for transfers between devices, padded_2(): before = lax.ppermute(last, axis, up)  25.5 us
    ppermute x8, waiting for transfers between devices, padded_2(): after = lax.ppermute(first, axis, down)  25.2 us
    div x2, other arithmetic, on_device(): quotient = recorded / blurred  11.9 us
    ppermute x8, starting transfers between devices, padded_2(): after = lax.ppermute(first, axis, down)  10.5 us
  transfers between devices with their start and end apart: 18, of which 15 were waited for; matrix products, arithmetic and copies ran while one was open for 5% of the time, Pallas kernels for 0%

profile of v1, /device:TPU:0, one launch (start us, length us, event | category | flops | bytes accessed | tf_op | source)
XLA Modules:
  0.0 296.6 jit_solution(13065002100297404981)
XLA Ops:
  6.5 1.2 fusion.415
  7.7 4.9 %collective-permute-start = (f32[15,16,256]{2,1,0:T(8,128)S(1)}, f32[15,16,256]{2,1,0:T(8,128)S(1)}, u32[]{:S(2)}, u32[]{:S(2)}) collective-permute-start(f32[15,16,256]{2,1,0:T(8,128)S(1)} %get-tuple-element.21), channel_id=1, source_target_pairs={{0,2},{2,4},{4,6},{6,8},{8,10},{10,12},{12,14},{1,3},{3,5},{5,7},{... | collective-permute-start | bytes 737288 | tf_op jit(solution)/shard_map/ppermute | solution.py:19
  12.6 1.3 collective-permute-start.1
  13.9 1.3 reduce_sum.45
  15.2 1.3 reduce_sum.47
  16.5 0.7 reverse.9
  17.3 0.7 reverse.11
  18.0 1.3 broadcast_divide_fusion
  19.3 0.7 fusion.422
  20.0 1.3 broadcast_divide_fusion.4
  21.3 0.7 fusion.423
  22.0 1.3 reduce_sum.46
  23.3 0.7 reverse.10
  24.0 1.3 broadcast_divide_fusion.2
  25.7 23.5 %fusion.378 = f32[64,16,256]{2,1,0:T(8,128)S(1)} fusion(f32[79,16,256]{2,1,0:T(8,128)S(1)} %constant_dynamic-update-slice_fusion.2, f32[79,16,256]{2,1,0:T(8,128)S(1)} %get-tuple-element.19, f32[64,16,256]{2,1,0:T(8,128)S(1)} %copy-done, f32[]{:T(128)} %bitcast.39, f32[]{:T(128)} %bitcast.38, f32[]{:T(128)} %bitcast.37, f32[]{:T(128)} %bitcast.36, ...), kind=kLoop, calls=%fused_computation.617 | loop fusion | flops 15990784 | bytes 33554556 | tf_op jit(solution)/shard_map/add | solution.py:33
  49.3 3.4 %collective-permute-start.2 = (f32[64,3,256]{2,1,0:T(4,128)S(1)}, f32[64,3,256]{2,1,0:T(4,128)S(1)}, u32[]{:S(2)}, u32[]{:S(2)}) collective-permute-start(f32[64,3,256]{2,1,0:T(4,128)S(1)} %get-tuple-element.17), channel_id=1, source_target_pairs={{0,1},{2,3},{4,5},{6,7},{8,9},{10,11},{12,13},{14,15},{16,17},{18,... | collective-permute-start | bytes 589832 | tf_op jit(solution)/shard_map/ppermute | solution.py:19
  52.7 1.3 collective-permute-start.3
  54.0 0.7 fusion.421
  54.7 0.7 fusion.420
  55.3 2.6 collective-permute-done.2
  57.9 4.1 %collective-permute-done.3 = f32[64,3,256]{2,1,0:T(4,128)S(1)} collective-permute-done((f32[64,3,256]{2,1,0:T(4,128)S(1)}, f32[64,3,256]{2,1,0:T(4,128)S(1)}, u32[]{:S(2)}, u32[]{:S(2)}) %collective-permute-start.3) | collective-permute-done | bytes 196640 | tf_op jit(solution)/shard_map/ppermute | solution.py:20
  62.1 5.6 %fusion.45 = f32[64,16,256]{2,1,0:T(8,128)S(1)} fusion(f32[64,16,256]{2,1,0:T(8,128)S(1)} %fusion.378, f32[64,3,256]{2,1,0:T(4,128)S(1)} %collective-permute-done.3, f32[64,3,256]{2,1,0:T(4,128)S(1)} %collective-permute-done.2, f32[]{:T(128)} %bitcast.45, f32[]{:T(128)} %bitcast.44, f32[]{:T(128)} %bitcast.43, f32[]{:T(128)} %bitcast.42, f32[]{:T(128)} %bitcast.41, ...), kind=kLoop, calls=%fused_computation.269 | loop fusion | flops 4980736 | bytes 2490396 | tf_op jit(solution)/shard_map/add | solution.py:33
  67.7 6.0 %fusion.321 = f32[64,16,256]{2,1,0:T(8,128)S(1)} fusion(f32[64,16,256]{2,1,0:T(8,128)S(1)} %fusion.45, f32[1,64,16,256]{3,2,1,0:T(8,128)S(1)} %copy-done.1, f32[]{:T(128)} %bitcast.51, f32[]{:T(128)} %bitcast.50, f32[]{:T(128)} %bitcast.49, f32[]{:T(128)} %bitcast.48, f32[]{:T(128)} %bitcast.47, f32[]{:T(128)} %bitcast.46, f32[]{:T(128)} %bitcast.7), kind=kLoop, calls=%fused_computation.545 | loop fusion | flops 3670016 | bytes 3145756 | tf_op jit(solution)/shard_map/div | solution.py:55
  73.7 4.3 %collective-permute-start.4 = (f32[15,16,256]{2,1,0:T(8,128)S(1)}, f32[15,16,256]{2,1,0:T(8,128)S(1)}, u32[]{:S(2)}, u32[]{:S(2)}) collective-permute-start(f32[15,16,256]{2,1,0:T(8,128)S(1)} %get-tuple-element.15), channel_id=1, source_target_pairs={{0,2},{2,4},{4,6},{6,8},{8,10},{10,12},{12,14},{1,3},{3,5},{5,7},{... | collective-permute-start | bytes 737288 | tf_op jit(solution)/shard_map/ppermute | solution.py:19
  78.0 1.3 collective-permute-start.5
  79.3 0.7 fusion.419
  80.0 0.7 fusion.418
  80.7 3.6 %collective-permute-done.4 = f32[15,16,256]{2,1,0:T(8,128)S(1)} collective-permute-done((f32[15,16,256]{2,1,0:T(8,128)S(1)}, f32[15,16,256]{2,1,0:T(8,128)S(1)}, u32[]{:S(2)}, u32[]{:S(2)}) %collective-permute-start.4) | collective-permute-done | bytes 245792 | tf_op jit(solution)/shard_map/ppermute | solution.py:19
  84.3 2.1 collective-permute-done.5
  86.4 23.6 %fusion.231 = f32[64,16,256]{2,1,0:T(8,128)S(1)} fusion(f32[64,16,256]{2,1,0:T(8,128)S(1)} %fusion.321, f32[15,16,256]{2,1,0:T(8,128)S(1)} %collective-permute-done.5, f32[15,16,256]{2,1,0:T(8,128)S(1)} %collective-permute-done.4, f32[]{:T(128)} %bitcast.81, f32[]{:T(128)} %bitcast.80, f32[]{:T(128)} %bitcast.79, f32[]{:T(128)} %bitcast.78, f32[]{:T(128)} %bitcast.77, ...), kind=kLoop, calls=%fused_computation.455 | loop fusion | flops 23855104 | bytes 2588796 | tf_op jit(solution)/shard_map/add | solution.py:33
  110.2 1.5 collective-permute-start.6
  111.6 1.3 collective-permute-start.7
  112.9 0.7 fusion.417
  113.6 0.7 fusion.416
  114.3 1.2 collective-permute-done.6
  115.5 4.4 %collective-permute-done.7 = f32[64,3,256]{2,1,0:T(4,128)S(1)} collective-permute-done((f32[64,3,256]{2,1,0:T(4,128)S(1)}, f32[64,3,256]{2,1,0:T(4,128)S(1)}, u32[]{:S(2)}, u32[]{:S(2)}) %collective-permute-start.7) | collective-permute-done | bytes 196640 | tf_op jit(solution)/shard_map/ppermute | solution.py:20
  119.9 5.4 %fusion.31 = f32[64,16,256]{2,1,0:T(8,128)S(1)} fusion(f32[64,16,256]{2,1,0:T(8,128)S(1)} %fusion.231, f32[64,3,256]{2,1,0:T(4,128)S(1)} %collective-permute-done.7, f32[64,3,256]{2,1,0:T(4,128)S(1)} %collective-permute-done.6, f32[]{:T(128)} %bitcast.87, f32[]{:T(128)} %bitcast.86, f32[]{:T(128)} %bitcast.85, f32[]{:T(128)} %bitcast.84, f32[]{:T(128)} %bitcast.83, ...), kind=kLoop, calls=%fused_computation.255 | loop fusion | flops 4980736 | bytes 2490396 | tf_op jit(solution)/shard_map/add | solution.py:33
  125.3 7.0 %fusion.333 = f32[64,16,256]{2,1,0:T(8,128)} fusion(f32[64,16,256]{2,1,0:T(8,128)S(1)} %fusion.31, f32[]{:T(128)} %bitcast.93, f32[]{:T(128)} %bitcast.92, f32[]{:T(128)} %bitcast.91, f32[]{:T(128)} %bitcast.90, f32[]{:T(128)} %bitcast.89, f32[]{:T(128)} %bitcast.88, f32[]{:T(128)} %bitcast.1), kind=kLoop, calls=%fused_computation.557 | loop fusion | flops 3407872 | bytes 2097180 | tf_op jit(solution)/shard_map/add | solution.py:33
  132.6 14.5 %all-gather.5.cloned.1.call-done = f32[128,16,256]{2,1,0:T(8,128)} async-done(((f32[64,16,256]{2,1,0:T(8,128)}), f32[128,16,256]{2,1,0:T(8,128)}) %all-gather.5.cloned.1.call-update) | async-done | bytes 2097168 | tf_op jit(solution)/shard_map/all_gather | solution.py:57
  147.1 1.9 reduce_sum.48
  149.2 3.7 %collective-permute-start.8 = (f32[15,16,256]{2,1,0:T(8,128)S(1)}, f32[15,16,256]{2,1,0:T(8,128)S(1)}, u32[]{:S(2)}, u32[]{:S(2)}) collective-permute-start(f32[15,16,256]{2,1,0:T(8,128)S(1)} %get-tuple-element.11), channel_id=1, source_target_pairs={{0,2},{2,4},{4,6},{6,8},{8,10},{10,12},{12,14},{1,3},{3,5},{5,7},{... | collective-permute-start | bytes 737288 | tf_op jit(solution)/shard_map/ppermute | solution.py:19
  152.9 1.3 collective-permute-start.9
  154.2 9.6 %collective-permute-done.8 = f32[15,16,256]{2,1,0:T(8,128)S(1)} collective-permute-done((f32[15,16,256]{2,1,0:T(8,128)S(1)}, f32[15,16,256]{2,1,0:T(8,128)S(1)}, u32[]{:S(2)}, u32[]{:S(2)}) %collective-permute-start.8) | collective-permute-done | bytes 245792 | tf_op jit(solution)/shard_map/ppermute | solution.py:19
  163.8 23.7 %fusion.145 = f32[64,16,256]{2,1,0:T(8,128)S(1)} fusion(f32[64,16,256]{2,1,0:T(8,128)S(1)} %multiply_multiply_fusion.1, f32[15,16,256]{2,1,0:T(8,128)S(1)} %collective-permute-done.9, f32[15,16,256]{2,1,0:T(8,128)S(1)} %collective-permute-done.8, f32[]{:T(128)} %bitcast.39, f32[]{:T(128)} %bitcast.38, f32[]{:T(128)} %bitcast.37, f32[]{:T(128)} %bitcast.36, ...), kind=kLoop, calls=%fused_computation.369 | loop fusion | flops 23855104 | bytes 2588796 | tf_op jit(solution)/shard_map/add | solution.py:33
  187.6 3.4 %collective-permute-start.10 = (f32[64,3,256]{2,1,0:T(4,128)S(1)}, f32[64,3,256]{2,1,0:T(4,128)S(1)}, u32[]{:S(2)}, u32[]{:S(2)}) collective-permute-start(f32[64,3,256]{2,1,0:T(4,128)S(1)} %get-tuple-element.9), channel_id=1, source_target_pairs={{0,1},{2,3},{4,5},{6,7},{8,9},{10,11},{12,13},{14,15},{16,17},{18,... | collective-permute-start | bytes 589832 | tf_op jit(solution)/shard_map/ppermute | solution.py:19
  191.0 1.4 collective-permute-start.11
  192.4 3.5 %collective-permute-done.10 = f32[64,3,256]{2,1,0:T(4,128)S(1)} collective-permute-done((f32[64,3,256]{2,1,0:T(4,128)S(1)}, f32[64,3,256]{2,1,0:T(4,128)S(1)}, u32[]{:S(2)}, u32[]{:S(2)}) %collective-permute-start.10) | collective-permute-done | bytes 196640 | tf_op jit(solution)/shard_map/ppermute | solution.py:19
  196.0 4.3 %collective-permute-done.11 = f32[64,3,256]{2,1,0:T(4,128)S(1)} collective-permute-done((f32[64,3,256]{2,1,0:T(4,128)S(1)}, f32[64,3,256]{2,1,0:T(4,128)S(1)}, u32[]{:S(2)}, u32[]{:S(2)}) %collective-permute-start.11) | collective-permute-done | bytes 196640 | tf_op jit(solution)/shard_map/ppermute | solution.py:20
  200.3 5.5 %fusion.17 = f32[64,16,256]{2,1,0:T(8,128)S(1)} fusion(f32[64,16,256]{2,1,0:T(8,128)S(1)} %fusion.145, f32[64,3,256]{2,1,0:T(4,128)S(1)} %collective-permute-done.11, f32[64,3,256]{2,1,0:T(4,128)S(1)} %collective-permute-done.10, f32[]{:T(128)} %bitcast.45, f32[]{:T(128)} %bitcast.44, f32[]{:T(128)} %bitcast.43, f32[]{:T(128)} %bitcast.42, f32[]{:T(128)} %bitcast.41, ...), kind=kLoop, calls=%fused_computation.241 | loop fusion | flops 4980736 | bytes 2490396 | tf_op jit(solution)/shard_map/add | solution.py:33
  205.8 6.0 %fusion.346 = f32[64,16,256]{2,1,0:T(8,128)S(1)} fusion(f32[64,16,256]{2,1,0:T(8,128)S(1)} %fusion.17, f32[1,64,16,256]{3,2,1,0:T(8,128)S(1)} %copy-done.2, f32[]{:T(128)} %bitcast.51, f32[]{:T(128)} %bitcast.50, f32[]{:T(128)} %bitcast.49, f32[]{:T(128)} %bitcast.48, f32[]{:T(128)} %bitcast.47, f32[]{:T(128)} %bitcast.46, f32[]{:T(128)} %bitcast.7), kind=kLoop, calls=%fused_computation.570 | loop fusion | flops 3670016 | bytes 3145756 | tf_op jit(solution)/shard_map/div | solution.py:55
  211.8 4.5 %collective-permute-start.12 = (f32[15,16,256]{2,1,0:T(8,128)S(1)}, f32[15,16,256]{2,1,0:T(8,128)S(1)}, u32[]{:S(2)}, u32[]{:S(2)}) collective-permute-start(f32[15,16,256]{2,1,0:T(8,128)S(1)} %get-tuple-element.7), channel_id=1, source_target_pairs={{0,2},{2,4},{4,6},{6,8},{8,10},{10,12},{12,14},{1,3},{3,5},{5,7},{... | collective-permute-start | bytes 737288 | tf_op jit(solution)/shard_map/ppermute | solution.py:19
  216.3 1.3 collective-permute-start.13
  217.6 2.4 collective-permute-done.12
  220.0 5.9 %collective-permute-done.13 = f32[15,16,256]{2,1,0:T(8,128)S(1)} collective-permute-done((f32[15,16,256]{2,1,0:T(8,128)S(1)}, f32[15,16,256]{2,1,0:T(8,128)S(1)}, u32[]{:S(2)}, u32[]{:S(2)}) %collective-permute-start.13) | collective-permute-done | bytes 245792 | tf_op jit(solution)/shard_map/ppermute | solution.py:20
  225.9 23.6 %fusion.59 = f32[64,16,256]{2,1,0:T(8,128)S(1)} fusion(f32[64,16,256]{2,1,0:T(8,128)S(1)} %fusion.346, f32[15,16,256]{2,1,0:T(8,128)S(1)} %collective-permute-done.13, f32[15,16,256]{2,1,0:T(8,128)S(1)} %collective-permute-done.12, f32[]{:T(128)} %bitcast.81, f32[]{:T(128)} %bitcast.80, f32[]{:T(128)} %bitcast.79, f32[]{:T(128)} %bitcast.78, f32[]{:T(128)} %bitcast.77, ...), kind=kLoop, calls=%fused_computation.283 | loop fusion | flops 23855104 | bytes 2588796 | tf_op jit(solution)/shard_map/add | solution.py:33
  249.6 1.5 collective-permute-start.14
  251.1 1.3 collective-permute-start.15
  252.4 2.6 collective-permute-done.14
  254.9 4.4 %collective-permute-done.15 = f32[64,3,256]{2,1,0:T(4,128)S(1)} collective-permute-done((f32[64,3,256]{2,1,0:T(4,128)S(1)}, f32[64,3,256]{2,1,0:T(4,128)S(1)}, u32[]{:S(2)}, u32[]{:S(2)}) %collective-permute-start.15) | collective-permute-done | bytes 196640 | tf_op jit(solution)/shard_map/ppermute | solution.py:20
  259.4 5.4 %fusion.3 = f32[64,16,256]{2,1,0:T(8,128)S(1)} fusion(f32[64,16,256]{2,1,0:T(8,128)S(1)} %fusion.59, f32[64,3,256]{2,1,0:T(4,128)S(1)} %collective-permute-done.15, f32[64,3,256]{2,1,0:T(4,128)S(1)} %collective-permute-done.14, f32[]{:T(128)} %bitcast.87, f32[]{:T(128)} %bitcast.86, f32[]{:T(128)} %bitcast.85, f32[]{:T(128)} %bitcast.84, f32[]{:T(128)} %bitcast.83, ...), kind=kLoop, calls=%fused_computation.227 | loop fusion | flops 4980736 | bytes 2490396 | tf_op jit(solution)/shard_map/add | solution.py:33
  264.8 7.0 %fusion.358 = f32[64,16,256]{2,1,0:T(8,128)} fusion(f32[64,16,256]{2,1,0:T(8,128)S(1)} %fusion.3, f32[]{:T(128)} %bitcast.93, f32[]{:T(128)} %bitcast.92, f32[]{:T(128)} %bitcast.91, f32[]{:T(128)} %bitcast.90, f32[]{:T(128)} %bitcast.89, f32[]{:T(128)} %bitcast.88, f32[]{:T(128)} %bitcast.1), kind=kLoop, calls=%fused_computation.582 | loop fusion | flops 3407872 | bytes 2097180 | tf_op jit(solution)/shard_map/add | solution.py:33
  271.8 14.8 %all-gather.7.cloned.1.call-done = f32[128,16,256]{2,1,0:T(8,128)} async-done(((f32[64,16,256]{2,1,0:T(8,128)}), f32[128,16,256]{2,1,0:T(8,128)}) %all-gather.7.cloned.1.call-update) | async-done | bytes 2097168 | tf_op jit(solution)/shard_map/all_gather | solution.py:57
  286.6 1.9 reduce_sum.49
  288.5 1.2 multiply_multiply_fusion
  (24 shorter events, 1.3 us)
Async XLA Ops:
  6.5 18.8 %copy-start = (f32[64,16,256]{2,1,0:T(8,128)S(1)}, f32[64,16,256]{2,1,0:T(8,128)}, u32[]{:S(2)}) copy-start(f32[64,16,256]{2,1,0:T(8,128)} %param.6) | copy-start | bytes 3145732
  6.5 140.5 %all-gather.5.cloned.1.call-start = ((), (), s32[]{:S(2)}) async-start(), calls=%async_computation | async-start | bytes 3145728 | tf_op jit(solution)/shard_map/all_gather | solution.py:57
  7.7 17.6 %collective-permute-start = (f32[15,16,256]{2,1,0:T(8,128)S(1)}, f32[15,16,256]{2,1,0:T(8,128)S(1)}, u32[]{:S(2)}, u32[]{:S(2)}) collective-permute-start(f32[15,16,256]{2,1,0:T(8,128)S(1)} %get-tuple-element.21), channel_id=1, source_target_pairs={{0,2},{2,4},{4,6},{6,8},{8,10},{10,12},{12,14},{1,3},{3,5},{5,7},{... | collective-permute-start | bytes 737288 | tf_op jit(solution)/shard_map/ppermute | solution.py:19
  12.6 13.0 %collective-permute-start.1 = (f32[15,16,256]{2,1,0:T(8,128)S(1)}, f32[15,16,256]{2,1,0:T(8,128)S(1)}, u32[]{:S(2)}, u32[]{:S(2)}) collective-permute-start(f32[15,16,256]{2,1,0:T(8,128)S(1)} %get-tuple-element.22), channel_id=1, source_target_pairs={{2,0},{4,2},{6,4},{8,6},{10,8},{12,10},{14,12},{3,1},{5,3},{7,5},{... | collective-permute-start | bytes 737288 | tf_op jit(solution)/shard_map/ppermute | solution.py:20
  49.3 8.7 %collective-permute-start.2 = (f32[64,3,256]{2,1,0:T(4,128)S(1)}, f32[64,3,256]{2,1,0:T(4,128)S(1)}, u32[]{:S(2)}, u32[]{:S(2)}) collective-permute-start(f32[64,3,256]{2,1,0:T(4,128)S(1)} %get-tuple-element.17), channel_id=1, source_target_pairs={{0,1},{2,3},{4,5},{6,7},{8,9},{10,11},{12,13},{14,15},{16,17},{18,... | collective-permute-start | bytes 589832 | tf_op jit(solution)/shard_map/ppermute | solution.py:19
  52.7 9.4 %collective-permute-start.3 = (f32[64,3,256]{2,1,0:T(4,128)S(1)}, f32[64,3,256]{2,1,0:T(4,128)S(1)}, u32[]{:S(2)}, u32[]{:S(2)}) collective-permute-start(f32[64,3,256]{2,1,0:T(4,128)S(1)} %get-tuple-element.18), channel_id=1, source_target_pairs={{1,0},{3,2},{5,4},{7,6},{9,8},{11,10},{13,12},{15,14},{17,16},{19,... | collective-permute-start | bytes 589832 | tf_op jit(solution)/shard_map/ppermute | solution.py:20
  62.1 5.6 %copy-start.1 = (f32[1,64,16,256]{3,2,1,0:T(8,128)S(1)}, f32[1,64,16,256]{3,2,1,0:T(8,128)}, u32[]{:S(2)}) copy-start(f32[1,64,16,256]{3,2,1,0:T(8,128)} %param.5) | copy-start | bytes 3145732
  73.7 10.6 %collective-permute-start.4 = (f32[15,16,256]{2,1,0:T(8,128)S(1)}, f32[15,16,256]{2,1,0:T(8,128)S(1)}, u32[]{:S(2)}, u32[]{:S(2)}) collective-permute-start(f32[15,16,256]{2,1,0:T(8,128)S(1)} %get-tuple-element.15), channel_id=1, source_target_pairs={{0,2},{2,4},{4,6},{6,8},{8,10},{10,12},{12,14},{1,3},{3,5},{5,7},{... | collective-permute-start | bytes 737288 | tf_op jit(solution)/shard_map/ppermute | solution.py:19
  78.0 8.5 %collective-permute-start.5 = (f32[15,16,256]{2,1,0:T(8,128)S(1)}, f32[15,16,256]{2,1,0:T(8,128)S(1)}, u32[]{:S(2)}, u32[]{:S(2)}) collective-permute-start(f32[15,16,256]{2,1,0:T(8,128)S(1)} %get-tuple-element.16), channel_id=1, source_target_pairs={{2,0},{4,2},{6,4},{8,6},{10,8},{12,10},{14,12},{3,1},{5,3},{7,5},{... | collective-permute-start | bytes 737288 | tf_op jit(solution)/shard_map/ppermute | solution.py:20
  110.2 5.3 %collective-permute-start.6 = (f32[64,3,256]{2,1,0:T(4,128)S(1)}, f32[64,3,256]{2,1,0:T(4,128)S(1)}, u32[]{:S(2)}, u32[]{:S(2)}) collective-permute-start(f32[64,3,256]{2,1,0:T(4,128)S(1)} %get-tuple-element.13), channel_id=1, source_target_pairs={{0,1},{2,3},{4,5},{6,7},{8,9},{10,11},{12,13},{14,15},{16,17},{18,... | collective-permute-start | bytes 589832 | tf_op jit(solution)/shard_map/ppermute | solution.py:19
  111.6 8.3 %collective-permute-start.7 = (f32[64,3,256]{2,1,0:T(4,128)S(1)}, f32[64,3,256]{2,1,0:T(4,128)S(1)}, u32[]{:S(2)}, u32[]{:S(2)}) collective-permute-start(f32[64,3,256]{2,1,0:T(4,128)S(1)} %get-tuple-element.14), channel_id=1, source_target_pairs={{1,0},{3,2},{5,4},{7,6},{9,8},{11,10},{13,12},{15,14},{17,16},{19,... | collective-permute-start | bytes 589832 | tf_op jit(solution)/shard_map/ppermute | solution.py:20
  132.3 154.3 %all-gather.7.cloned.1.call-start = ((), (), s32[]{:S(2)}) async-start(), calls=%async_computation.1 | async-start | bytes 3145728 | tf_op jit(solution)/shard_map/all_gather | solution.py:57
  149.2 14.6 %collective-permute-start.8 = (f32[15,16,256]{2,1,0:T(8,128)S(1)}, f32[15,16,256]{2,1,0:T(8,128)S(1)}, u32[]{:S(2)}, u32[]{:S(2)}) collective-permute-start(f32[15,16,256]{2,1,0:T(8,128)S(1)} %get-tuple-element.11), channel_id=1, source_target_pairs={{0,2},{2,4},{4,6},{6,8},{8,10},{10,12},{12,14},{1,3},{3,5},{5,7},{... | collective-permute-start | bytes 737288 | tf_op jit(solution)/shard_map/ppermute | solution.py:19
  152.9 10.9 %collective-permute-start.9 = (f32[15,16,256]{2,1,0:T(8,128)S(1)}, f32[15,16,256]{2,1,0:T(8,128)S(1)}, u32[]{:S(2)}, u32[]{:S(2)}) collective-permute-start(f32[15,16,256]{2,1,0:T(8,128)S(1)} %get-tuple-element.12), channel_id=1, source_target_pairs={{2,0},{4,2},{6,4},{8,6},{10,8},{12,10},{14,12},{3,1},{5,3},{7,5},{... | collective-permute-start | bytes 737288 | tf_op jit(solution)/shard_map/ppermute | solution.py:20
  187.6 8.4 %collective-permute-start.10 = (f32[64,3,256]{2,1,0:T(4,128)S(1)}, f32[64,3,256]{2,1,0:T(4,128)S(1)}, u32[]{:S(2)}, u32[]{:S(2)}) collective-permute-start(f32[64,3,256]{2,1,0:T(4,128)S(1)} %get-tuple-element.9), channel_id=1, source_target_pairs={{0,1},{2,3},{4,5},{6,7},{8,9},{10,11},{12,13},{14,15},{16,17},{18,... | collective-permute-start | bytes 589832 | tf_op jit(solution)/shard_map/ppermute | solution.py:19
  191.0 14.8 %copy-start.2 = (f32[1,64,16,256]{3,2,1,0:T(8,128)S(1)}, f32[1,64,16,256]{3,2,1,0:T(8,128)}, u32[]{:S(2)}) copy-start(f32[1,64,16,256]{3,2,1,0:T(8,128)} %param.5) | copy-start | bytes 3145732
  191.0 9.2 %collective-permute-start.11 = (f32[64,3,256]{2,1,0:T(4,128)S(1)}, f32[64,3,256]{2,1,0:T(4,128)S(1)}, u32[]{:S(2)}, u32[]{:S(2)}) collective-permute-start(f32[64,3,256]{2,1,0:T(4,128)S(1)} %get-tuple-element.10), channel_id=1, source_target_pairs={{1,0},{3,2},{5,4},{7,6},{9,8},{11,10},{13,12},{15,14},{17,16},{19,... | collective-permute-start | bytes 589832 | tf_op jit(solution)/shard_map/ppermute | solution.py:20
  211.8 8.2 %collective-permute-start.12 = (f32[15,16,256]{2,1,0:T(8,128)S(1)}, f32[15,16,256]{2,1,0:T(8,128)S(1)}, u32[]{:S(2)}, u32[]{:S(2)}) collective-permute-start(f32[15,16,256]{2,1,0:T(8,128)S(1)} %get-tuple-element.7), channel_id=1, source_target_pairs={{0,2},{2,4},{4,6},{6,8},{8,10},{10,12},{12,14},{1,3},{3,5},{5,7},{... | collective-permute-start | bytes 737288 | tf_op jit(solution)/shard_map/ppermute | solution.py:19
  216.3 9.6 %collective-permute-start.13 = (f32[15,16,256]{2,1,0:T(8,128)S(1)}, f32[15,16,256]{2,1,0:T(8,128)S(1)}, u32[]{:S(2)}, u32[]{:S(2)}) collective-permute-start(f32[15,16,256]{2,1,0:T(8,128)S(1)} %get-tuple-element.8), channel_id=1, source_target_pairs={{2,0},{4,2},{6,4},{8,6},{10,8},{12,10},{14,12},{3,1},{5,3},{7,5},{... | collective-permute-start | bytes 737288 | tf_op jit(solution)/shard_map/ppermute | solution.py:20
  249.6 5.3 %collective-permute-start.14 = (f32[64,3,256]{2,1,0:T(4,128)S(1)}, f32[64,3,256]{2,1,0:T(4,128)S(1)}, u32[]{:S(2)}, u32[]{:S(2)}) collective-permute-start(f32[64,3,256]{2,1,0:T(4,128)S(1)} %get-tuple-element.5), channel_id=1, source_target_pairs={{0,1},{2,3},{4,5},{6,7},{8,9},{10,11},{12,13},{14,15},{16,17},{18,... | collective-permute-start | bytes 589832 | tf_op jit(solution)/shard_map/ppermute | solution.py:19
  251.1 8.3 %collective-permute-start.15 = (f32[64,3,256]{2,1,0:T(4,128)S(1)}, f32[64,3,256]{2,1,0:T(4,128)S(1)}, u32[]{:S(2)}, u32[]{:S(2)}) collective-permute-start(f32[64,3,256]{2,1,0:T(4,128)S(1)} %get-tuple-element.6), channel_id=1, source_target_pairs={{1,0},{3,2},{5,4},{7,6},{9,8},{11,10},{13,12},{15,14},{17,16},{19,... | collective-permute-start | bytes 589832 | tf_op jit(solution)/shard_map/ppermute | solution.py:20
Sparse Core Ops, SparseCore 0:
  132.5 14.5 all-gather.4
  271.9 14.6 all-gather.6
